TPU v7x, 512 devices: a whole 4x8x8 slice. The times are simulated.
512 devices in a mesh: ha: 8 (over y_lo, core), az: 64 (over x, z, y_hi).
Axes of the slice: x: 4, y: 8 (y_hi: 2, y_lo: 4; y = y_hi * 4 + y_lo), z: 8, core: 2. Of those that a mesh axis runs over, the one named last changes fastest.
Arguments:
- field: float32 [2, 4096, 8192], P(None, 'ha', 'az'), may hold values from -6 to 6
- terrain: int32 [8192], P('az'), may hold values from 0 to 63
- profile_pick: int32 [8192], P('az'), may hold values from 0 to 15
- profile_table: float32 [16, 4096], replicated, may hold values from -3.140625 to 3.140625
- clutter_mask: int32 [128, 8192], P(None, 'az'), may hold values 0 or 1
- pulse: float32 [63], replicated, may hold values from -0.6 to 0.6
- beam: float32 [31], replicated, may hold values from -0.9 to 0.9
- measured: float32 [2, 128, 8192], P(None, None, 'az'), may hold values from -6 to 6
Outputs:
- field_out: float32 [2, 4096, 8192], P(None, 'ha', 'az')
- sources: float32 [2, 2, 128, 8192], P(None, None, 'ha', 'az')
All inputs are finite; a program needn't handle non-finite values. No bound on the sum of `clutter_mask` on one device may be relied on, other than what follows from the above.
Results may differ from a plain program's by a relative error of at most 0.00022.
Values sent between devices are 32-bit elements; how exact they have to be, the bound alone decides.
No kernel may reach another device: no remote copies, remote signals or barrier semaphores. Data moves between devices by JAX's collectives and lax.ppermute only.
A program may use at most 64 MiB of HBM per device.

v0:
```python
import math
import jax
import jax.numpy as jnp
from jax import lax
from jax.sharding import PartitionSpec as P

height_chirp = 1
azimuth_chirp = 3


def broadcast(block, axis, owner):
    block = jnp.where(lax.axis_index(axis) == owner, block, jnp.zeros_like(block))
    return lax.psum(block, axis)


def with_halo(cells, sides, width):
    for axis, dim in sides:
        count = lax.axis_size(axis)
        head = lax.slice_in_dim(cells, 0, width, axis=dim)
        tail = lax.slice_in_dim(cells, cells.shape[dim] - width, cells.shape[dim], axis=dim)
        cells = jnp.concatenate(
            [
                lax.ppermute(tail, axis, [(i, (i + 1) % count) for i in range(count)]),
                cells,
                lax.ppermute(head, axis, [((i + 1) % count, i) for i in range(count)]),
            ],
            axis=dim,
        )
    return cells


def factors(count):
    first = 1
    probe = 1
    while probe * probe <= count:
        if count % probe == 0:
            first = probe
        probe += 1
    return (first, count // first)


def unit_roots(rows, cols, modulus):
    left = lax.broadcasted_iota(jnp.int32, (rows, cols), 0)
    right = lax.broadcasted_iota(jnp.int32, (rows, cols), 1)
    turn = (left * right % modulus).astype(jnp.float32) * (2.0 * math.pi / modulus)
    return (jnp.cos(turn), -jnp.sin(turn))


def chirp_table(first, second, spread, count):
    low = lax.broadcasted_iota(jnp.int32, (first, second), 0)
    high = lax.broadcasted_iota(jnp.int32, (first, second), 1)
    index = low + first * high
    angle = (spread * index * index % (2 * count)).astype(jnp.float32) * (-math.pi / count)
    return (jnp.cos(angle), jnp.sin(angle))


def complex_table(table_re, table_im):
    return jnp.stack([jnp.stack([table_re, -table_im]), jnp.stack([table_im, table_re])])


def cmul(left_re, left_im, right_re, right_im):
    return (left_re * right_re - left_im * right_im, left_re * right_im + left_im * right_re)


def stacked_mul(vals, table_re, table_im):
    new_re, new_im = cmul(vals[0], vals[1], table_re, table_im)
    return jnp.stack([new_re, new_im])


def propagate(part_re, part_im, spread):
    highest = lax.Precision.HIGHEST
    count = part_re.shape[1]
    first, second = factors(count)
    split = (part_re.shape[0], first, second)
    table_shape = (1, first, second)
    outer_re, outer_im = unit_roots(first, first, first)
    inner_re, inner_im = unit_roots(second, second, second)
    twist_re, twist_im = unit_roots(first, second, count)
    twist_re = twist_re.reshape(table_shape)
    twist_im = twist_im.reshape(table_shape)
    phase_re, phase_im = chirp_table(first, second, spread, count)
    phase_re = phase_re.reshape(table_shape)
    phase_im = phase_im.reshape(table_shape)
    outer_fwd = complex_table(outer_re, outer_im)
    inner_fwd = complex_table(inner_re, inner_im)
    inner_inv = complex_table(inner_re.T, -inner_im.T)
    outer_inv = complex_table(outer_re.T, -outer_im.T)
    vals = jnp.stack([part_re.reshape(split), part_im.reshape(split)])
    vals = jnp.einsum("ocka,clab->olkb", outer_fwd, vals, precision=highest)
    vals = stacked_mul(vals, twist_re, twist_im)
    vals = jnp.einsum("clkb,ocbq->olkq", vals, inner_fwd, precision=highest)
    vals = stacked_mul(vals, phase_re, phase_im)
    vals = jnp.einsum("clkq,ocqb->olkb", vals, inner_inv, precision=highest)
    vals = stacked_mul(vals, twist_re, -twist_im)
    vals = jnp.einsum("ocak,clkb->olab", outer_inv, vals, precision=highest)
    scale = 1.0 / count
    return ((vals[0] * scale).reshape(part_re.shape), (vals[1] * scale).reshape(part_im.shape))


def screen_coef(rows, terr, phase, total):
    height = rows.astype(jnp.float32)
    depth = jnp.maximum(height - 0.75 * total, 0.0) / (0.25 * total)
    amount = jnp.exp(-4.0 * depth * depth) * (rows >= terr).astype(jnp.float32)
    return (amount * jnp.cos(phase), amount * jnp.sin(phase))


def onehot_of(picks, count):
    return (picks[None, :] == lax.broadcasted_iota(jnp.int32, (count, picks.shape[0]), 0)).astype(
        jnp.float32
    )


def lookup(table, picks):
    return jnp.einsum(
        "pr,pc->rc", table, onehot_of(picks, table.shape[0]), precision=lax.Precision.HIGHEST
    )


def band(taps, offset):
    hit = offset[:, :, None] == lax.broadcasted_iota(jnp.int32, (1, 1, taps.shape[0]), 2)
    return jnp.sum(jnp.where(hit, taps[None, None, :], 0.0), axis=-1)


def apply_screen(wave, coef):
    new_re, new_im = cmul(wave[0], wave[1], coef[0], coef[1])
    return jnp.stack([new_re, new_im])


def turn_rows(rows):
    new_re, new_im = propagate(rows[0], rows[1], azimuth_chirp)
    return jnp.stack([new_re, new_im])


def turn_items(block):
    return turn_rows(block[:, 0])[:, None]


def to_rows(wave):
    n_az = lax.axis_size("az")
    h_dev = wave.shape[1]
    part_rows = h_dev // n_az
    shaped = wave.reshape(2, n_az, part_rows, wave.shape[2])
    moved = turn_items(lax.all_to_all(shaped, "az", split_axis=1, concat_axis=3, tiled=True))
    return moved.reshape(2, part_rows, moved.shape[3])


def rows_to_slab(rows):
    return lax.all_to_all(rows, "az", split_axis=2, concat_axis=1, tiled=True)


def across(wave):
    return rows_to_slab(to_rows(wave))


def to_tall(wave):
    flipped = jnp.swapaxes(wave, 1, 2)
    return lax.all_to_all(flipped, "ha", split_axis=1, concat_axis=2, tiled=True)


def to_slab(tall):
    flipped = lax.all_to_all(tall, "ha", split_axis=2, concat_axis=1, tiled=True)
    return jnp.swapaxes(flipped, 1, 2)


def down(tall):
    new_re, new_im = propagate(tall[0], tall[1], height_chirp)
    return jnp.stack([new_re, new_im])


def root_strip(wave, bottom):
    return broadcast(wave[:, :bottom, :], "ha", 0)


def beam_forward(values, half_beam, forward_band):
    wider = with_halo(values, (("az", 1),), half_beam)
    return jnp.dot(wider, forward_band, precision=lax.Precision.HIGHEST)


def beam_backward(values, half_beam, back_band):
    wider = with_halo(values, (("az", 1),), half_beam)
    return jnp.dot(wider, back_band, precision=lax.Precision.HIGHEST)


def local(field, terrain, profile_pick, profile_table, clutter_mask, pulse, beam, measured):
    highest = lax.Precision.HIGHEST
    n_slabs = lax.axis_size("ha")
    h_dev = field.shape[1]
    a_dev = field.shape[2]
    total_h = h_dev * n_slabs
    slab = lax.axis_index("ha")
    bottom = clutter_mask.shape[0]
    share_rows = bottom // n_slabs
    row_start = slab * share_rows
    mask = clutter_mask.astype(jnp.float32)
    taps_range = pulse.shape[0]
    half_range = (taps_range - 1) // 2
    row_grid = lax.broadcasted_iota(jnp.int32, (bottom, bottom), 0)
    col_grid = lax.broadcasted_iota(jnp.int32, (bottom, bottom), 1)
    rmat = band(pulse, col_grid - row_grid + half_range)
    half_beam = (beam.shape[0] - 1) // 2
    wide = a_dev + 2 * half_beam
    edge = lax.broadcasted_iota(jnp.int32, (wide, a_dev), 0)
    column = lax.broadcasted_iota(jnp.int32, (wide, a_dev), 1)
    forward_band = band(beam, edge - column)
    back_band = band(beam, column - edge + 2 * half_beam)
    slab_rows = slab * h_dev + lax.broadcasted_iota(jnp.int32, (h_dev, 1), 0)
    slab_phase = lookup(
        lax.dynamic_slice_in_dim(profile_table, slab * h_dev, h_dev, 1), profile_pick
    )
    slab_coef = screen_coef(slab_rows, terrain[None, :], slab_phase, total_h)
    steps_count = measured.shape[0]
    wave = field
    result = []
    for step in range(steps_count):
        wave = to_slab(down(to_tall(across(wave))))
        wave = apply_screen(wave, slab_coef)
        strip = root_strip(wave, bottom)
        low_re = strip[0]
        low_im = strip[1]
        power = mask * (low_re * low_re + low_im * low_im)
        target = measured[step]
        ranged = jnp.dot(rmat, power, precision=highest)
        model = beam_forward(ranged, half_beam, forward_band)
        misfit = model - target
        spread_back = beam_backward(misfit, half_beam, back_band)
        back = jnp.einsum("pr,pa->ra", rmat, spread_back, precision=highest)
        whole = jnp.stack([2.0 * mask * low_re * back, 2.0 * mask * low_im * back])
        result.append(lax.dynamic_slice_in_dim(whole, row_start, share_rows, 1))
    return (wave, jnp.stack(result))


def solution(mesh):
    return jax.shard_map(
        local,
        mesh=mesh,
        in_specs=(
            P(None, "ha", "az"),
            P("az"),
            P("az"),
            P(),
            P(None, "az"),
            P(),
            P(),
            P(None, None, "az"),
        ),
        out_specs=(P(None, "ha", "az"), P(None, None, "ha", "az")),
        check_vma=False,
    )
```

profile of v0, /device:TPU:8, one launch (start us, length us, event | category | flops | bytes accessed | tf_op | source)
XLA Modules:
  0.0 512.8 jit_solution(6664515977165057099)
XLA Ops:
  7.2 1.9 copy.267
  9.1 18.1 %all-to-all-start = ((f32[2,64,8,128]{3,2,0,1:T(8,128)}), f32[2,64,8,128]{3,2,0,1:T(8,128)S(1)}, u32[]{:S(2)}, u32[]{:S(2)}) async-start(f32[2,64,8,128]{3,2,0,1:T(8,128)} %copy.267), calls=%async_computation | async-start | bytes 1048576 | tf_op jit(solution)/shard_map/all_to_all | solution.py:143
  28.6 21.4 %all-to-all-done = f32[2,64,8,128]{3,2,0,1:T(8,128)S(1)} async-done(((f32[2,64,8,128]{3,2,0,1:T(8,128)}), f32[2,64,8,128]{3,2,0,1:T(8,128)S(1)}, u32[]{:S(2)}, u32[]{:S(2)}) %all-to-all-start) | async-done | bytes 524320 | tf_op jit(solution)/shard_map/all_to_all | solution.py:143
  53.2 7.7 %copy.272 = f32[2,8,8192]{1,0,2:T(2,128)} copy(f32[2,8,8192]{2,1,0:T(8,128)S(1)} %pad_maximum_fusion.1) | data formatting | bytes 1048576 | tf_op jit(solution)/shard_map/stack | solution.py:131
  60.9 13.0 %reshape.559 = f32[64,1,2048]{2,1,0:T(1,128)S(1)} reshape(f32[8192,2,8]{2,1,0:T(2,128)} %bitcast.382) | data formatting | bytes 1048576
  73.8 27.5 %all_to_all.132 = f32[64,1,2048]{2,1,0:T(1,128)S(1)} all-to-all(f32[64,1,2048]{2,1,0:T(1,128)S(1)} %reshape.559), channel_id=1, replica_groups=mesh['ha'=8,'az'=64] {'az'}, dimensions={0} | all-to-all | bytes 1048576 | tf_op jit(solution)/shard_map/all_to_all | solution.py:148
  101.9 1.9 reduce
  103.8 14.1 %reshape.560 = f32[8192,2,8]{2,1,0:T(2,128)} reshape(f32[64,2048]{1,0:T(8,128)S(1)} %reduce) | data formatting | bytes 1048576
  117.9 9.2 %copy.365 = f32[2,8,64,128]{3,1,2,0:T(8,128)S(1)} copy(f32[2,8,64,128]{1,0,3,2:T(2,128)} %bitcast.383) | data formatting | bytes 1048576 | tf_op jit(solution)/shard_map/all_to_all | solution.py:148
  128.0 3.4 all-to-all-start.2
  132.0 11.4 %all-to-all-done.2 = f32[2,128,512]{2,0,1:T(2,128)S(1)} async-done(((f32[2,128,512]{2,0,1:T(2,128)}), f32[2,128,512]{2,0,1:T(2,128)S(1)}, u32[]{:S(2)}, u32[]{:S(2)}) %all-to-all-start.2) | async-done | bytes 524320 | tf_op jit(solution)/shard_map/all_to_all | solution.py:157
  150.2 4.4 copy.288
  154.6 7.9 %reshape.561 = f32[8,1,16384]{2,1,0:T(1,128)} reshape(f32[4096,2,16]{2,1,0:T(2,128)} %bitcast.386) | data formatting | bytes 1048576
  162.4 7.1 %all-to-all-start.3 = ((f32[8,1,16384]{2,1,0:T(1,128)}), f32[8,1,16384]{2,1,0:T(1,128)S(1)}, u32[]{:S(2)}, u32[]{:S(2)}) async-start(f32[8,1,16384]{2,1,0:T(1,128)} %reshape.561), calls=%async_computation.3 | async-start | bytes 1048576 | tf_op jit(solution)/shard_map/all_to_all | solution.py:161
  169.5 12.1 %all-to-all-done.3 = f32[8,1,16384]{2,1,0:T(1,128)S(1)} async-done(((f32[8,1,16384]{2,1,0:T(1,128)}), f32[8,1,16384]{2,1,0:T(1,128)S(1)}, u32[]{:S(2)}, u32[]{:S(2)}) %all-to-all-start.3) | async-done | bytes 524320 | tf_op jit(solution)/shard_map/all_to_all | solution.py:161
  181.6 1.9 reduce.1
  183.5 7.6 %reshape.562 = f32[4096,2,16]{2,1,0:T(2,128)} reshape(f32[8,16384]{1,0:T(8,128)S(1)} %reduce.1) | data formatting | bytes 1048576
  191.1 5.1 copy.371
  196.5 1.3 multiply_subtract_fusion.9
  197.8 26.0 %all_to_all.133 = f32[2,64,8,128]{3,2,0,1:T(8,128)S(1)} all-to-all(f32[2,64,8,128]{3,2,0,1:T(8,128)S(1)} %pad_maximum_fusion.3), channel_id=1, replica_groups=mesh['ha'=8,'az'=64] {'az'}, dimensions={1} | all-to-all | bytes 1048576 | tf_op jit(solution)/shard_map/all_to_all | solution.py:143
  227.0 7.7 %copy.298 = f32[2,8,8192]{1,0,2:T(2,128)} copy(f32[2,8,8192]{2,1,0:T(8,128)S(1)} %pad_maximum_fusion.4) | data formatting | bytes 1048576 | tf_op jit(solution)/shard_map/stack | solution.py:131
  234.7 13.0 %reshape.563 = f32[64,1,2048]{2,1,0:T(1,128)S(1)} reshape(f32[8192,2,8]{2,1,0:T(2,128)} %bitcast.384) | data formatting | bytes 1048576
  247.7 30.4 %all_to_all.134 = f32[64,1,2048]{2,1,0:T(1,128)S(1)} all-to-all(f32[64,1,2048]{2,1,0:T(1,128)S(1)} %reshape.563), channel_id=1, replica_groups=mesh['ha'=8,'az'=64] {'az'}, dimensions={0} | all-to-all | bytes 1048576 | tf_op jit(solution)/shard_map/all_to_all | solution.py:148
  278.1 1.9 reduce.2
  280.0 14.1 %reshape.564 = f32[8192,2,8]{2,1,0:T(2,128)} reshape(f32[64,2048]{1,0:T(8,128)S(1)} %reduce.2) | data formatting | bytes 1048576
  294.1 9.2 %copy.376 = f32[2,8,64,128]{3,1,2,0:T(8,128)S(1)} copy(f32[2,8,64,128]{1,0,3,2:T(2,128)} %bitcast.385) | data formatting | bytes 1048576 | tf_op jit(solution)/shard_map/all_to_all | solution.py:148
  303.5 17.0 %all_to_all.135 = f32[2,128,512]{2,0,1:T(2,128)S(1)} all-to-all(f32[2,128,512]{2,0,1:T(2,128)S(1)} %copy.301), channel_id=1, replica_groups=mesh['ha'=8,'az'=64] {'ha'}, dimensions={1} | all-to-all | bytes 1048576 | tf_op jit(solution)/shard_map/all_to_all | solution.py:157
  324.1 1.1 convolution_bitcast_fusion.1
  327.2 4.4 copy.314
  331.6 7.9 %reshape.565 = f32[8,1,16384]{2,1,0:T(1,128)} reshape(f32[4096,2,16]{2,1,0:T(2,128)} %bitcast.388) | data formatting | bytes 1048576
  339.5 5.7 %all-to-all-start.7 = ((f32[8,1,16384]{2,1,0:T(1,128)}), f32[8,1,16384]{2,1,0:T(1,128)S(1)}, u32[]{:S(2)}, u32[]{:S(2)}) async-start(f32[8,1,16384]{2,1,0:T(1,128)} %reshape.565), calls=%async_computation.7 | async-start | bytes 1048576 | tf_op jit(solution)/shard_map/all_to_all | solution.py:161
  347.0 10.4 %all-to-all-done.7 = f32[8,1,16384]{2,1,0:T(1,128)S(1)} async-done(((f32[8,1,16384]{2,1,0:T(1,128)}), f32[8,1,16384]{2,1,0:T(1,128)S(1)}, u32[]{:S(2)}, u32[]{:S(2)}) %all-to-all-start.7) | async-done | bytes 524320 | tf_op jit(solution)/shard_map/all_to_all | solution.py:161
  357.3 1.9 reduce.3
  359.2 7.6 %reshape.566 = f32[4096,2,16]{2,1,0:T(2,128)} reshape(f32[8,16384]{1,0:T(8,128)S(1)} %reduce.3) | data formatting | bytes 1048576
  366.8 5.2 %copy.382 = f32[2,16,8,512]{3,1,2,0:T(8,128)S(1)} copy(f32[2,16,8,512]{1,0,3,2:T(2,128)} %bitcast.389) | data formatting | bytes 1048576 | tf_op jit(solution)/shard_map/all_to_all | solution.py:161
  372.2 1.4 subtract_bitcast_fusion
  375.6 67.0 %all-reduce.3.cloned.1.call-done = (f32[2,128,128]{2,1,0:T(8,128)}, f32[2,128,128]{2,1,0:T(8,128)}) async-done(((f32[2,128,128]{2,1,0:T(8,128)}, f32[2,128,128]{2,1,0:T(8,128)}), (f32[2,128,128]{2,1,0:T(8,128)}, f32[2,128,128]{2,1,0:T(8,128)})) %all-reduce.3.cloned.1.call-update) | async-done | bytes 262160 | tf_op jit(solution)/shard_map/psum | solution.py:13
  442.6 1.2 fusion.70
  443.8 1.2 fusion.75
  444.9 4.6 collective-permute-start
  449.6 9.3 %collective-permute-start.1 = (f32[128,15]{0,1:T(8,128)S(1)}, f32[128,15]{0,1:T(8,128)S(1)}, u32[]{:S(2)}, u32[]{:S(2)}) collective-permute-start(f32[128,15]{0,1:T(8,128)S(1)} %get-tuple-element.65), channel_id=1, source_target_pairs={{1,0},{2,1},{3,2},{4,3},{5,4},{6,5},{7,6},{8,7},{9,8},{10,9},{11,1... | collective-permute-start | bytes 23048 | tf_op jit(solution)/shard_map/ppermute | solution.py:25
  458.9 1.9 collective-permute-start.4
  460.9 12.0 %collective-permute-start.5 = (f32[128,15]{0,1:T(8,128)S(1)}, f32[128,15]{0,1:T(8,128)S(1)}, u32[]{:S(2)}, u32[]{:S(2)}) collective-permute-start(f32[128,15]{0,1:T(8,128)S(1)} %get-tuple-element.69), channel_id=1, source_target_pairs={{1,0},{2,1},{3,2},{4,3},{5,4},{6,5},{7,6},{8,7},{9,8},{10,9},{11,1... | collective-permute-start | bytes 23048 | tf_op jit(solution)/shard_map/ppermute | solution.py:25
  473.4 1.9 collective-permute-start.2
  475.3 12.0 %collective-permute-start.3 = (f32[128,15]{0,1:T(8,128)S(1)}, f32[128,15]{0,1:T(8,128)S(1)}, u32[]{:S(2)}, u32[]{:S(2)}) collective-permute-start(f32[128,15]{0,1:T(8,128)S(1)} %get-tuple-element.63), channel_id=1, source_target_pairs={{1,0},{2,1},{3,2},{4,3},{5,4},{6,5},{7,6},{8,7},{9,8},{10,9},{11,1... | collective-permute-start | bytes 23048 | tf_op jit(solution)/shard_map/ppermute | solution.py:25
  487.9 1.9 collective-permute-start.6
  489.8 12.0 %collective-permute-start.7 = (f32[128,15]{0,1:T(8,128)S(1)}, f32[128,15]{0,1:T(8,128)S(1)}, u32[]{:S(2)}, u32[]{:S(2)}) collective-permute-start(f32[128,15]{0,1:T(8,128)S(1)} %get-tuple-element.67), channel_id=1, source_target_pairs={{1,0},{2,1},{3,2},{4,3},{5,4},{6,5},{7,6},{8,7},{9,8},{10,9},{11,1... | collective-permute-start | bytes 23048 | tf_op jit(solution)/shard_map/ppermute | solution.py:25
  503.6 1.2 multiply_bitcast_fusion.2
  (137 shorter events, 29.4 us)
Async XLA Ops:
  7.2 189.3 %copy-start = (f32[16,4096]{1,0:T(8,128)S(1)}, f32[16,4096]{1,0:T(8,128)}, u32[]{:S(2)}) copy-start(f32[16,4096]{1,0:T(8,128)} %param.11) | copy-start | bytes 786436
  9.1 40.9 %all-to-all-start = ((f32[2,64,8,128]{3,2,0,1:T(8,128)}), f32[2,64,8,128]{3,2,0,1:T(8,128)S(1)}, u32[]{:S(2)}, u32[]{:S(2)}) async-start(f32[2,64,8,128]{3,2,0,1:T(8,128)} %copy.267), calls=%async_computation | async-start | bytes 1048576 | tf_op jit(solution)/shard_map/all_to_all | solution.py:143
  128.0 15.4 %all-to-all-start.2 = ((f32[2,128,512]{2,0,1:T(2,128)}), f32[2,128,512]{2,0,1:T(2,128)S(1)}, u32[]{:S(2)}, u32[]{:S(2)}) async-start(f32[2,128,512]{2,0,1:T(2,128)} %copy.275), calls=%async_computation.2 | async-start | bytes 1048576 | tf_op jit(solution)/shard_map/all_to_all | solution.py:157
  162.4 19.2 %all-to-all-start.3 = ((f32[8,1,16384]{2,1,0:T(1,128)}), f32[8,1,16384]{2,1,0:T(1,128)S(1)}, u32[]{:S(2)}, u32[]{:S(2)}) async-start(f32[8,1,16384]{2,1,0:T(1,128)} %reshape.561), calls=%async_computation.3 | async-start | bytes 1048576 | tf_op jit(solution)/shard_map/all_to_all | solution.py:161
  183.5 12.9 %copy-start.4 = (s32[128]{0:T(128)S(1)}, s32[128]{0:T(128)}, u32[]{:S(2)}) copy-start(s32[128]{0:T(128)} %param.9) | copy-start | bytes 1540
  183.5 12.9 %copy-start.5 = (s32[128]{0:T(128)S(1)}, s32[128]{0:T(128)}, u32[]{:S(2)}) copy-start(s32[128]{0:T(128)} %param.10) | copy-start | bytes 1540
  327.2 18.2 %copy-start.3 = (f32[2,128,128]{2,1,0:T(8,128)S(1)}, f32[2,128,128]{2,1,0:T(8,128)}, u32[]{:S(2)}) copy-start(f32[2,128,128]{2,1,0:T(8,128)} %param.15) | copy-start | bytes 393220
  331.6 14.1 %copy-start.6 = (f32[31]{0:T(128)S(1)}, f32[31]{0:T(128)}, u32[]{:S(2)}) copy-start(f32[31]{0:T(128)} %param.14) | copy-start | bytes 376
  339.5 17.8 %all-to-all-start.7 = ((f32[8,1,16384]{2,1,0:T(1,128)}), f32[8,1,16384]{2,1,0:T(1,128)S(1)}, u32[]{:S(2)}, u32[]{:S(2)}) async-start(f32[8,1,16384]{2,1,0:T(1,128)} %reshape.565), calls=%async_computation.7 | async-start | bytes 1048576 | tf_op jit(solution)/shard_map/all_to_all | solution.py:161
  345.2 97.4 %all-reduce.3.cloned.1.call-start = ((), (), s32[]{:S(2)}) async-start(), calls=%async_computation.8 | async-start | bytes 524288 | tf_op jit(solution)/shard_map/psum | solution.py:13
  366.8 7.5 %copy-start.7 = (f32[63]{0:T(128)S(1)}, f32[63]{0:T(128)}, u32[]{:S(2)}) copy-start(f32[63]{0:T(128)} %param.13) | copy-start | bytes 760
  366.8 75.8 %copy-start.2 = (s32[128,128]{1,0:T(8,128)S(1)}, s32[128,128]{1,0:T(8,128)}, u32[]{:S(2)}) copy-start(s32[128,128]{1,0:T(8,128)} %param.12) | copy-start | bytes 196612
  366.8 138.7 %copy-start.1 = (f32[16,4096]{1,0:T(8,128)S(1)}, f32[16,4096]{1,0:T(8,128)}, u32[]{:S(2)}) copy-start(f32[16,4096]{1,0:T(8,128)} %param.11) | copy-start | bytes 786436
  444.9 28.0 %collective-permute-start = (f32[128,15]{0,1:T(8,128)S(1)}, f32[128,15]{0,1:T(8,128)S(1)}, u32[]{:S(2)}, u32[]{:S(2)}) collective-permute-start(f32[128,15]{0,1:T(8,128)S(1)} %get-tuple-element.64), channel_id=1, source_target_pairs={{0,1},{1,2},{2,3},{3,4},{4,5},{5,6},{6,7},{7,8},{8,9},{9,10},{10,1... | collective-permute-start | bytes 23048 | tf_op jit(solution)/shard_map/ppermute | solution.py:23
  449.6 23.4 %collective-permute-start.1 = (f32[128,15]{0,1:T(8,128)S(1)}, f32[128,15]{0,1:T(8,128)S(1)}, u32[]{:S(2)}, u32[]{:S(2)}) collective-permute-start(f32[128,15]{0,1:T(8,128)S(1)} %get-tuple-element.65), channel_id=1, source_target_pairs={{1,0},{2,1},{3,2},{4,3},{5,4},{6,5},{7,6},{8,7},{9,8},{10,9},{11,1... | collective-permute-start | bytes 23048 | tf_op jit(solution)/shard_map/ppermute | solution.py:25
  458.9 28.5 %collective-permute-start.4 = (f32[128,15]{0,1:T(8,128)S(1)}, f32[128,15]{0,1:T(8,128)S(1)}, u32[]{:S(2)}, u32[]{:S(2)}) collective-permute-start(f32[128,15]{0,1:T(8,128)S(1)} %get-tuple-element.68), channel_id=1, source_target_pairs={{0,1},{1,2},{2,3},{3,4},{4,5},{5,6},{6,7},{7,8},{8,9},{9,10},{10,1... | collective-permute-start | bytes 23048 | tf_op jit(solution)/shard_map/ppermute | solution.py:23
  460.9 26.5 %collective-permute-start.5 = (f32[128,15]{0,1:T(8,128)S(1)}, f32[128,15]{0,1:T(8,128)S(1)}, u32[]{:S(2)}, u32[]{:S(2)}) collective-permute-start(f32[128,15]{0,1:T(8,128)S(1)} %get-tuple-element.69), channel_id=1, source_target_pairs={{1,0},{2,1},{3,2},{4,3},{5,4},{6,5},{7,6},{8,7},{9,8},{10,9},{11,1... | collective-permute-start | bytes 23048 | tf_op jit(solution)/shard_map/ppermute | solution.py:25
  473.4 28.4 %collective-permute-start.2 = (f32[128,15]{0,1:T(8,128)S(1)}, f32[128,15]{0,1:T(8,128)S(1)}, u32[]{:S(2)}, u32[]{:S(2)}) collective-permute-start(f32[128,15]{0,1:T(8,128)S(1)} %get-tuple-element.62), channel_id=1, source_target_pairs={{0,1},{1,2},{2,3},{3,4},{4,5},{5,6},{6,7},{7,8},{8,9},{9,10},{10,1... | collective-permute-start | bytes 23048 | tf_op jit(solution)/shard_map/ppermute | solution.py:23
  475.3 26.5 %collective-permute-start.3 = (f32[128,15]{0,1:T(8,128)S(1)}, f32[128,15]{0,1:T(8,128)S(1)}, u32[]{:S(2)}, u32[]{:S(2)}) collective-permute-start(f32[128,15]{0,1:T(8,128)S(1)} %get-tuple-element.63), channel_id=1, source_target_pairs={{1,0},{2,1},{3,2},{4,3},{5,4},{6,5},{7,6},{8,7},{9,8},{10,9},{11,1... | collective-permute-start | bytes 23048 | tf_op jit(solution)/shard_map/ppermute | solution.py:25
  487.9 14.7 %collective-permute-start.6 = (f32[128,15]{0,1:T(8,128)S(1)}, f32[128,15]{0,1:T(8,128)S(1)}, u32[]{:S(2)}, u32[]{:S(2)}) collective-permute-start(f32[128,15]{0,1:T(8,128)S(1)} %get-tuple-element.66), channel_id=1, source_target_pairs={{0,1},{1,2},{2,3},{3,4},{4,5},{5,6},{6,7},{7,8},{8,9},{9,10},{10,1... | collective-permute-start | bytes 23048 | tf_op jit(solution)/shard_map/ppermute | solution.py:23
  489.8 13.4 %collective-permute-start.7 = (f32[128,15]{0,1:T(8,128)S(1)}, f32[128,15]{0,1:T(8,128)S(1)}, u32[]{:S(2)}, u32[]{:S(2)}) collective-permute-start(f32[128,15]{0,1:T(8,128)S(1)} %get-tuple-element.67), channel_id=1, source_target_pairs={{1,0},{2,1},{3,2},{4,3},{5,4},{6,5},{7,6},{8,7},{9,8},{10,9},{11,1... | collective-permute-start | bytes 23048 | tf_op jit(solution)/shard_map/ppermute | solution.py:25
Sparse Core Ops, SparseCore 0:
  374.4 68.1 all-reduce.2
where the time goes:
time: 522 us; the launch traced here: 513 us
  local copies, waits for them, and re-layouts  146 us (28%)
  waiting for transfers between devices  123 us (24%)
  blocking collectives  101 us (19%)
  starting transfers between devices  90.5 us (17%)
  matrix products  20.1 us (4%)
  other arithmetic  16.4 us (3%)
  between operations  15.5 us (3%)
    unnamed x26, local copies, waits for them, and re-layouts  85.3 us
    psum x1, waiting for transfers between devices, broadcast(): return lax.psum(block, axis)  67 us
    all_to_all x2, blocking collectives, rows_to_slab(): return lax.all_to_all(rows, 'az', split_axis=2, concat_axis=1, tiled=True)  57.9 us
    ppermute x4, starting transfers between devices, with_halo(): lax.ppermute(head, axis, [((i + 1) % count, i) for i in range(count)])  45.5 us
    all_to_all x1, blocking collectives, to_rows(): lax.all_to_all(shaped, 'az', split_axis=1, concat_axis=3, tiled=True)  26 us
    all_to_all x2, waiting for transfers between devices, to_slab(): lax.all_to_all(tall, 'ha', split_axis=2, concat_axis=1, tiled=True)  22.4 us
    all_to_all x1, waiting for transfers between devices, to_rows(): lax.all_to_all(shaped, 'az', split_axis=1, concat_axis=3, tiled=True)  21.4 us
    all_to_all x3, local copies, waits for them, and re-layouts, rows_to_slab(): return lax.all_to_all(rows, 'az', split_axis=2, concat_axis=1, tiled=True)  18.8 us
  transfers between devices with their start and end apart: 13, of which 6 were waited for; matrix products, arithmetic and copies ran while one was open for 1% of the time, Pallas kernels for 0%

commit v1 on v0

--- a/solution.py
+++ b/solution.py
@@ -10,7 +10,7 @@
 
 def broadcast(block, axis, owner):
     block = jnp.where(lax.axis_index(axis) == owner, block, jnp.zeros_like(block))
-    return lax.psum(block, axis)
+    return jnp.sum(lax.all_gather(block, axis), axis=0)
 
 
 def with_halo(cells, sides, width):

time: 522 us -> 463 us (0.89)
  the two profiles are of different devices: /device:TPU:8 before, /device:TPU:24 now
where the time goes in v1:
time: 463 us; the launch traced here: 454 us
  local copies, waits for them, and re-layouts  147 us (32%)
  starting transfers between devices  103 us (22%)
  blocking collectives  80.1 us (17%)
  waiting for transfers between devices  71.1 us (15%)
  other arithmetic  19 us (4%)
  matrix products  17.4 us (4%)
  between operations  15.5 us (3%)
    unnamed x26, local copies, waits for them, and re-layouts  85.3 us
    all_to_all x2, blocking collectives, rows_to_slab(): return lax.all_to_all(rows, 'az', split_axis=2, concat_axis=1, tiled=True)  53.3 us
    ppermute x4, starting transfers between devices, with_halo(): lax.ppermute(head, axis, [((i + 1) % count, i) for i in range(count)])  46.8 us
    all_to_all x1, blocking collectives, to_rows(): lax.all_to_all(shaped, 'az', split_axis=1, concat_axis=3, tiled=True)  26.8 us
    all_to_all x2, waiting for transfers between devices, to_tall(): lax.all_to_all(flipped, 'ha', split_axis=1, concat_axis=2, tiled=True)  25.7 us
    all_to_all x2, waiting for transfers between devices, to_slab(): lax.all_to_all(tall, 'ha', split_axis=2, concat_axis=1, tiled=True)  25.2 us
    all_to_all x3, local copies, waits for them, and re-layouts, rows_to_slab(): return lax.all_to_all(rows, 'az', split_axis=2, concat_axis=1, tiled=True)  18.8 us
    all_to_all x2, starting transfers between devices, to_tall(): lax.all_to_all(flipped, 'ha', split_axis=1, concat_axis=2, tiled=True)  17.3 us
  transfers between devices with their start and end apart: 15, of which 9 were waited for; matrix products, arithmetic and copies ran while one was open for 9% of the time, Pallas kernels for 0%

profile of v1, /device:TPU:24, one launch (start us, length us, event | category | flops | bytes accessed | tf_op | source)
XLA Modules:
  0.0 453.9 jit_solution(9957482894521365410)
XLA Ops:
  7.2 1.9 copy.267
  9.1 16.3 %all-to-all-start = ((f32[2,64,8,128]{3,2,0,1:T(8,128)}), f32[2,64,8,128]{3,2,0,1:T(8,128)S(1)}, u32[]{:S(2)}, u32[]{:S(2)}) async-start(f32[2,64,8,128]{3,2,0,1:T(8,128)} %copy.267), calls=%async_computation | async-start | bytes 1048576 | tf_op jit(solution)/shard_map/all_to_all | solution.py:143
  26.8 16.1 %all-to-all-done = f32[2,64,8,128]{3,2,0,1:T(8,128)S(1)} async-done(((f32[2,64,8,128]{3,2,0,1:T(8,128)}), f32[2,64,8,128]{3,2,0,1:T(8,128)S(1)}, u32[]{:S(2)}, u32[]{:S(2)}) %all-to-all-start) | async-done | bytes 524320 | tf_op jit(solution)/shard_map/all_to_all | solution.py:143
  46.1 7.7 %copy.272 = f32[2,8,8192]{1,0,2:T(2,128)} copy(f32[2,8,8192]{2,1,0:T(8,128)S(1)} %pad_maximum_fusion.1) | data formatting | bytes 1048576 | tf_op jit(solution)/shard_map/stack | solution.py:131
  53.8 13.0 %reshape.561 = f32[64,1,2048]{2,1,0:T(1,128)S(1)} reshape(f32[8192,2,8]{2,1,0:T(2,128)} %bitcast.384) | data formatting | bytes 1048576
  66.8 27.4 %all_to_all.132 = f32[64,1,2048]{2,1,0:T(1,128)S(1)} all-to-all(f32[64,1,2048]{2,1,0:T(1,128)S(1)} %reshape.561), channel_id=1, replica_groups=mesh['ha'=8,'az'=64] {'az'}, dimensions={0} | all-to-all | bytes 1048576 | tf_op jit(solution)/shard_map/all_to_all | solution.py:148
  94.7 1.9 reduce
  96.6 14.1 %reshape.562 = f32[8192,2,8]{2,1,0:T(2,128)} reshape(f32[64,2048]{1,0:T(8,128)S(1)} %reduce) | data formatting | bytes 1048576
  110.7 9.2 %copy.365 = f32[2,8,64,128]{3,1,2,0:T(8,128)S(1)} copy(f32[2,8,64,128]{1,0,3,2:T(2,128)} %bitcast.385) | data formatting | bytes 1048576 | tf_op jit(solution)/shard_map/all_to_all | solution.py:148
  120.8 10.3 %all-to-all-start.2 = ((f32[2,128,512]{2,0,1:T(2,128)}), f32[2,128,512]{2,0,1:T(2,128)S(1)}, u32[]{:S(2)}, u32[]{:S(2)}) async-start(f32[2,128,512]{2,0,1:T(2,128)} %copy.275), calls=%async_computation.2 | async-start | bytes 1048576 | tf_op jit(solution)/shard_map/all_to_all | solution.py:157
  131.6 12.3 %all-to-all-done.2 = f32[2,128,512]{2,0,1:T(2,128)S(1)} async-done(((f32[2,128,512]{2,0,1:T(2,128)}), f32[2,128,512]{2,0,1:T(2,128)S(1)}, u32[]{:S(2)}, u32[]{:S(2)}) %all-to-all-start.2) | async-done | bytes 524320 | tf_op jit(solution)/shard_map/all_to_all | solution.py:157
  150.7 4.4 copy.288
  155.0 7.9 %reshape.563 = f32[8,1,16384]{2,1,0:T(1,128)} reshape(f32[4096,2,16]{2,1,0:T(2,128)} %bitcast.388) | data formatting | bytes 1048576
  162.9 6.4 %all-to-all-start.3 = ((f32[8,1,16384]{2,1,0:T(1,128)}), f32[8,1,16384]{2,1,0:T(1,128)S(1)}, u32[]{:S(2)}, u32[]{:S(2)}) async-start(f32[8,1,16384]{2,1,0:T(1,128)} %reshape.563), calls=%async_computation.3 | async-start | bytes 1048576 | tf_op jit(solution)/shard_map/all_to_all | solution.py:161
  169.3 12.7 %all-to-all-done.3 = f32[8,1,16384]{2,1,0:T(1,128)S(1)} async-done(((f32[8,1,16384]{2,1,0:T(1,128)}), f32[8,1,16384]{2,1,0:T(1,128)S(1)}, u32[]{:S(2)}, u32[]{:S(2)}) %all-to-all-start.3) | async-done | bytes 524320 | tf_op jit(solution)/shard_map/all_to_all | solution.py:161
  182.0 1.9 reduce.1
  183.9 7.6 %reshape.564 = f32[4096,2,16]{2,1,0:T(2,128)} reshape(f32[8,16384]{1,0:T(8,128)S(1)} %reduce.1) | data formatting | bytes 1048576
  191.5 5.1 %copy.371 = f32[2,16,8,512]{3,1,2,0:T(8,128)S(1)} copy(f32[2,16,8,512]{1,0,3,2:T(2,128)} %bitcast.389) | data formatting | bytes 1048576 | tf_op jit(solution)/shard_map/all_to_all | solution.py:161
  196.9 1.3 multiply_subtract_fusion.9
  198.3 26.8 %all_to_all.133 = f32[2,64,8,128]{3,2,0,1:T(8,128)S(1)} all-to-all(f32[2,64,8,128]{3,2,0,1:T(8,128)S(1)} %pad_maximum_fusion.3), channel_id=1, replica_groups=mesh['ha'=8,'az'=64] {'az'}, dimensions={1} | all-to-all | bytes 1048576 | tf_op jit(solution)/shard_map/all_to_all | solution.py:143
  228.3 7.7 %copy.298 = f32[2,8,8192]{1,0,2:T(2,128)} copy(f32[2,8,8192]{2,1,0:T(8,128)S(1)} %pad_maximum_fusion.4) | data formatting | bytes 1048576 | tf_op jit(solution)/shard_map/stack | solution.py:131
  236.0 13.0 %reshape.565 = f32[64,1,2048]{2,1,0:T(1,128)S(1)} reshape(f32[8192,2,8]{2,1,0:T(2,128)} %bitcast.386) | data formatting | bytes 1048576
  248.9 25.9 %all_to_all.134 = f32[64,1,2048]{2,1,0:T(1,128)S(1)} all-to-all(f32[64,1,2048]{2,1,0:T(1,128)S(1)} %reshape.565), channel_id=1, replica_groups=mesh['ha'=8,'az'=64] {'az'}, dimensions={0} | all-to-all | bytes 1048576 | tf_op jit(solution)/shard_map/all_to_all | solution.py:148
  274.8 1.9 reduce.2
  276.7 14.1 %reshape.566 = f32[8192,2,8]{2,1,0:T(2,128)} reshape(f32[64,2048]{1,0:T(8,128)S(1)} %reduce.2) | data formatting | bytes 1048576
  290.8 9.2 %copy.376 = f32[2,8,64,128]{3,1,2,0:T(8,128)S(1)} copy(f32[2,8,64,128]{1,0,3,2:T(2,128)} %bitcast.387) | data formatting | bytes 1048576 | tf_op jit(solution)/shard_map/all_to_all | solution.py:148
  301.0 7.0 %all-to-all-start.6 = ((f32[2,128,512]{2,0,1:T(2,128)}), f32[2,128,512]{2,0,1:T(2,128)S(1)}, u32[]{:S(2)}, u32[]{:S(2)}) async-start(f32[2,128,512]{2,0,1:T(2,128)} %copy.301), calls=%async_computation.6 | async-start | bytes 1048576 | tf_op jit(solution)/shard_map/all_to_all | solution.py:157
  308.9 13.5 %all-to-all-done.6 = f32[2,128,512]{2,0,1:T(2,128)S(1)} async-done(((f32[2,128,512]{2,0,1:T(2,128)}), f32[2,128,512]{2,0,1:T(2,128)S(1)}, u32[]{:S(2)}, u32[]{:S(2)}) %all-to-all-start.6) | async-done | bytes 524320 | tf_op jit(solution)/shard_map/all_to_all | solution.py:157
  329.1 4.4 copy.314
  333.5 7.9 %reshape.567 = f32[8,1,16384]{2,1,0:T(1,128)} reshape(f32[4096,2,16]{2,1,0:T(2,128)} %bitcast.390) | data formatting | bytes 1048576
  341.3 6.3 %all-to-all-start.7 = ((f32[8,1,16384]{2,1,0:T(1,128)}), f32[8,1,16384]{2,1,0:T(1,128)S(1)}, u32[]{:S(2)}, u32[]{:S(2)}) async-start(f32[8,1,16384]{2,1,0:T(1,128)} %reshape.567), calls=%async_computation.7 | async-start | bytes 1048576 | tf_op jit(solution)/shard_map/all_to_all | solution.py:161
  347.9 12.5 %all-to-all-done.7 = f32[8,1,16384]{2,1,0:T(1,128)S(1)} async-done(((f32[8,1,16384]{2,1,0:T(1,128)}), f32[8,1,16384]{2,1,0:T(1,128)S(1)}, u32[]{:S(2)}, u32[]{:S(2)}) %all-to-all-start.7) | async-done | bytes 524320 | tf_op jit(solution)/shard_map/all_to_all | solution.py:161
  360.4 1.9 reduce.3
  362.3 7.6 %reshape.568 = f32[4096,2,16]{2,1,0:T(2,128)} reshape(f32[8,16384]{1,0:T(8,128)S(1)} %reduce.3) | data formatting | bytes 1048576
  369.9 5.2 %copy.382 = f32[2,16,8,512]{3,1,2,0:T(8,128)S(1)} copy(f32[2,16,8,512]{1,0,3,2:T(2,128)} %bitcast.391) | data formatting | bytes 1048576 | tf_op jit(solution)/shard_map/all_to_all | solution.py:161
  375.3 1.4 subtract_bitcast_fusion
  378.5 1.3 reduce_sum.45
  380.1 1.9 collective-permute-start
  382.0 12.0 %collective-permute-start.1 = (f32[128,15]{0,1:T(8,128)S(1)}, f32[128,15]{0,1:T(8,128)S(1)}, u32[]{:S(2)}, u32[]{:S(2)}) collective-permute-start(f32[128,15]{0,1:T(8,128)S(1)} %get-tuple-element.63), channel_id=1, source_target_pairs={{1,0},{2,1},{3,2},{4,3},{5,4},{6,5},{7,6},{8,7},{9,8},{10,9},{11,1... | collective-permute-start | bytes 23048 | tf_op jit(solution)/shard_map/ppermute | solution.py:25
  394.2 1.2 collective-permute-done.1
  395.9 4.1 collective-permute-start.2
  400.0 10.1 %collective-permute-start.3 = (f32[128,15]{0,1:T(8,128)S(1)}, f32[128,15]{0,1:T(8,128)S(1)}, u32[]{:S(2)}, u32[]{:S(2)}) collective-permute-start(f32[128,15]{0,1:T(8,128)S(1)} %get-tuple-element.61), channel_id=1, source_target_pairs={{1,0},{2,1},{3,2},{4,3},{5,4},{6,5},{7,6},{8,7},{9,8},{10,9},{11,1... | collective-permute-start | bytes 23048 | tf_op jit(solution)/shard_map/ppermute | solution.py:25
  410.2 1.2 collective-permute-done.3
  411.9 1.3 reduce_sum.49
  413.5 1.9 collective-permute-start.4
  415.5 12.3 %collective-permute-start.5 = (f32[128,15]{0,1:T(8,128)S(1)}, f32[128,15]{0,1:T(8,128)S(1)}, u32[]{:S(2)}, u32[]{:S(2)}) collective-permute-start(f32[128,15]{0,1:T(8,128)S(1)} %get-tuple-element.67), channel_id=1, source_target_pairs={{1,0},{2,1},{3,2},{4,3},{5,4},{6,5},{7,6},{8,7},{9,8},{10,9},{11,1... | collective-permute-start | bytes 23048 | tf_op jit(solution)/shard_map/ppermute | solution.py:25
  429.6 1.9 collective-permute-start.6
  431.5 12.3 %collective-permute-start.7 = (f32[128,15]{0,1:T(8,128)S(1)}, f32[128,15]{0,1:T(8,128)S(1)}, u32[]{:S(2)}, u32[]{:S(2)}) collective-permute-start(f32[128,15]{0,1:T(8,128)S(1)} %get-tuple-element.65), channel_id=1, source_target_pairs={{1,0},{2,1},{3,2},{4,3},{5,4},{6,5},{7,6},{8,7},{9,8},{10,9},{11,1... | collective-permute-start | bytes 23048 | tf_op jit(solution)/shard_map/ppermute | solution.py:25
  (143 shorter events, 33.3 us)
Async XLA Ops:
  7.2 189.7 %copy-start = (f32[16,4096]{1,0:T(8,128)S(1)}, f32[16,4096]{1,0:T(8,128)}, u32[]{:S(2)}) copy-start(f32[16,4096]{1,0:T(8,128)} %param.11) | copy-start | bytes 786436
  9.1 33.9 %all-to-all-start = ((f32[2,64,8,128]{3,2,0,1:T(8,128)}), f32[2,64,8,128]{3,2,0,1:T(8,128)S(1)}, u32[]{:S(2)}, u32[]{:S(2)}) async-start(f32[2,64,8,128]{3,2,0,1:T(8,128)} %copy.267), calls=%async_computation | async-start | bytes 1048576 | tf_op jit(solution)/shard_map/all_to_all | solution.py:143
  120.8 23.1 %all-to-all-start.2 = ((f32[2,128,512]{2,0,1:T(2,128)}), f32[2,128,512]{2,0,1:T(2,128)S(1)}, u32[]{:S(2)}, u32[]{:S(2)}) async-start(f32[2,128,512]{2,0,1:T(2,128)} %copy.275), calls=%async_computation.2 | async-start | bytes 1048576 | tf_op jit(solution)/shard_map/all_to_all | solution.py:157
  162.9 19.1 %all-to-all-start.3 = ((f32[8,1,16384]{2,1,0:T(1,128)}), f32[8,1,16384]{2,1,0:T(1,128)S(1)}, u32[]{:S(2)}, u32[]{:S(2)}) async-start(f32[8,1,16384]{2,1,0:T(1,128)} %reshape.563), calls=%async_computation.3 | async-start | bytes 1048576 | tf_op jit(solution)/shard_map/all_to_all | solution.py:161
  183.9 12.9 %copy-start.4 = (s32[128]{0:T(128)S(1)}, s32[128]{0:T(128)}, u32[]{:S(2)}) copy-start(s32[128]{0:T(128)} %param.9) | copy-start | bytes 1540
  183.9 12.9 %copy-start.5 = (s32[128]{0:T(128)S(1)}, s32[128]{0:T(128)}, u32[]{:S(2)}) copy-start(s32[128]{0:T(128)} %param.10) | copy-start | bytes 1540
  301.0 21.3 %all-to-all-start.6 = ((f32[2,128,512]{2,0,1:T(2,128)}), f32[2,128,512]{2,0,1:T(2,128)S(1)}, u32[]{:S(2)}, u32[]{:S(2)}) async-start(f32[2,128,512]{2,0,1:T(2,128)} %copy.301), calls=%async_computation.6 | async-start | bytes 1048576 | tf_op jit(solution)/shard_map/all_to_all | solution.py:157
  308.0 70.5 %all-gather.5.cloned.1.call-start = ((), (), s32[]{:S(2)}) async-start(), calls=%async_computation.8 | async-start | bytes 1179648 | tf_op jit(solution)/shard_map/all_gather | solution.py:13
  341.3 19.1 %all-to-all-start.7 = ((f32[8,1,16384]{2,1,0:T(1,128)}), f32[8,1,16384]{2,1,0:T(1,128)S(1)}, u32[]{:S(2)}, u32[]{:S(2)}) async-start(f32[8,1,16384]{2,1,0:T(1,128)} %reshape.567), calls=%async_computation.7 | async-start | bytes 1048576 | tf_op jit(solution)/shard_map/all_to_all | solution.py:161
  347.6 64.3 %all-gather.7.cloned.1.call-start = ((), (), s32[]{:S(2)}) async-start(), calls=%async_computation.9 | async-start | bytes 1179648 | tf_op jit(solution)/shard_map/all_gather | solution.py:13
  369.9 7.5 %copy-start.6 = (f32[63]{0:T(128)S(1)}, f32[63]{0:T(128)}, u32[]{:S(2)}) copy-start(f32[63]{0:T(128)} %param.13) | copy-start | bytes 760
  369.9 8.0 %copy-start.7 = (f32[31]{0:T(128)S(1)}, f32[31]{0:T(128)}, u32[]{:S(2)}) copy-start(f32[31]{0:T(128)} %param.14) | copy-start | bytes 376
  369.9 9.9 %copy-start.2 = (s32[128,128]{1,0:T(8,128)S(1)}, s32[128,128]{1,0:T(8,128)}, u32[]{:S(2)}) copy-start(s32[128,128]{1,0:T(8,128)} %param.12) | copy-start | bytes 196612
  369.9 24.2 %copy-start.3 = (f32[2,128,128]{2,1,0:T(8,128)S(1)}, f32[2,128,128]{2,1,0:T(8,128)}, u32[]{:S(2)}) copy-start(f32[2,128,128]{2,1,0:T(8,128)} %param.15) | copy-start | bytes 393220
  375.3 71.3 %copy-start.1 = (f32[16,4096]{1,0:T(8,128)S(1)}, f32[16,4096]{1,0:T(8,128)}, u32[]{:S(2)}) copy-start(f32[16,4096]{1,0:T(8,128)} %param.11) | copy-start | bytes 786436
  380.1 14.1 %collective-permute-start = (f32[128,15]{0,1:T(8,128)S(1)}, f32[128,15]{0,1:T(8,128)S(1)}, u32[]{:S(2)}, u32[]{:S(2)}) collective-permute-start(f32[128,15]{0,1:T(8,128)S(1)} %get-tuple-element.62), channel_id=1, source_target_pairs={{0,1},{1,2},{2,3},{3,4},{4,5},{5,6},{6,7},{7,8},{8,9},{9,10},{10,1... | collective-permute-start | bytes 23048 | tf_op jit(solution)/shard_map/ppermute | solution.py:23
  382.0 13.4 %collective-permute-start.1 = (f32[128,15]{0,1:T(8,128)S(1)}, f32[128,15]{0,1:T(8,128)S(1)}, u32[]{:S(2)}, u32[]{:S(2)}) collective-permute-start(f32[128,15]{0,1:T(8,128)S(1)} %get-tuple-element.63), channel_id=1, source_target_pairs={{1,0},{2,1},{3,2},{4,3},{5,4},{6,5},{7,6},{8,7},{9,8},{10,9},{11,1... | collective-permute-start | bytes 23048 | tf_op jit(solution)/shard_map/ppermute | solution.py:25
  395.9 14.4 %collective-permute-start.2 = (f32[128,15]{0,1:T(8,128)S(1)}, f32[128,15]{0,1:T(8,128)S(1)}, u32[]{:S(2)}, u32[]{:S(2)}) collective-permute-start(f32[128,15]{0,1:T(8,128)S(1)} %get-tuple-element.60), channel_id=1, source_target_pairs={{0,1},{1,2},{2,3},{3,4},{4,5},{5,6},{6,7},{7,8},{8,9},{9,10},{10,1... | collective-permute-start | bytes 23048 | tf_op jit(solution)/shard_map/ppermute | solution.py:23
  400.0 11.5 %collective-permute-start.3 = (f32[128,15]{0,1:T(8,128)S(1)}, f32[128,15]{0,1:T(8,128)S(1)}, u32[]{:S(2)}, u32[]{:S(2)}) collective-permute-start(f32[128,15]{0,1:T(8,128)S(1)} %get-tuple-element.61), channel_id=1, source_target_pairs={{1,0},{2,1},{3,2},{4,3},{5,4},{6,5},{7,6},{8,7},{9,8},{10,9},{11,1... | collective-permute-start | bytes 23048 | tf_op jit(solution)/shard_map/ppermute | solution.py:25
  413.5 14.5 %collective-permute-start.4 = (f32[128,15]{0,1:T(8,128)S(1)}, f32[128,15]{0,1:T(8,128)S(1)}, u32[]{:S(2)}, u32[]{:S(2)}) collective-permute-start(f32[128,15]{0,1:T(8,128)S(1)} %get-tuple-element.66), channel_id=1, source_target_pairs={{0,1},{1,2},{2,3},{3,4},{4,5},{5,6},{6,7},{7,8},{8,9},{9,10},{10,1... | collective-permute-start | bytes 23048 | tf_op jit(solution)/shard_map/ppermute | solution.py:23
  415.5 13.7 %collective-permute-start.5 = (f32[128,15]{0,1:T(8,128)S(1)}, f32[128,15]{0,1:T(8,128)S(1)}, u32[]{:S(2)}, u32[]{:S(2)}) collective-permute-start(f32[128,15]{0,1:T(8,128)S(1)} %get-tuple-element.67), channel_id=1, source_target_pairs={{1,0},{2,1},{3,2},{4,3},{5,4},{6,5},{7,6},{8,7},{9,8},{10,9},{11,1... | collective-permute-start | bytes 23048 | tf_op jit(solution)/shard_map/ppermute | solution.py:25
  429.6 15.1 %collective-permute-start.6 = (f32[128,15]{0,1:T(8,128)S(1)}, f32[128,15]{0,1:T(8,128)S(1)}, u32[]{:S(2)}, u32[]{:S(2)}) collective-permute-start(f32[128,15]{0,1:T(8,128)S(1)} %get-tuple-element.64), channel_id=1, source_target_pairs={{0,1},{1,2},{2,3},{3,4},{4,5},{5,6},{6,7},{7,8},{8,9},{9,10},{10,1... | collective-permute-start | bytes 23048 | tf_op jit(solution)/shard_map/ppermute | solution.py:23
  431.5 13.7 %collective-permute-start.7 = (f32[128,15]{0,1:T(8,128)S(1)}, f32[128,15]{0,1:T(8,128)S(1)}, u32[]{:S(2)}, u32[]{:S(2)}) collective-permute-start(f32[128,15]{0,1:T(8,128)S(1)} %get-tuple-element.65), channel_id=1, source_target_pairs={{1,0},{2,1},{3,2},{4,3},{5,4},{6,5},{7,6},{8,7},{9,8},{10,9},{11,1... | collective-permute-start | bytes 23048 | tf_op jit(solution)/shard_map/ppermute | solution.py:25
Sparse Core Ops, SparseCore 0:
  310.8 29.5 all-gather.4
  377.5 28.5 all-gather.6
